TPU v7x, 32 devices: a whole 2x2x4 slice. The times are simulated.
32 devices in a mesh: dp: 16 (over z, y, core), tensor: 2 (over x).
Axes of the slice: x: 2, y: 2, z: 4, core: 2. Of those that a mesh axis runs over, the one named last changes fastest.
Arguments:
- inputs: bfloat16 [9216, 8192], P('dp', 'tensor'), may hold values from -6 to 6
- out_grads: bfloat16 [9216, 11264], P('dp', 'tensor'), may hold values from -600 to 600
- basis: bfloat16 [8192, 512], P('dp', 'tensor'), may hold values from -40 to 40
- weight: bfloat16 [8192, 11264], P('dp', 'tensor'), may hold values from -0.099609375 to 0.099609375
- first_moment: float32 [512, 11264], P('dp', 'tensor'), may hold values from -0.9 to 0.9
- second_moment: float32 [512, 11264], P('dp', 'tensor'), may hold values from 0.01 to 1
Outputs:
- new_weight: bfloat16 [8192, 11264], P('dp', 'tensor')
- new_first: float32 [512, 11264], P('dp', 'tensor')
- new_second: float32 [512, 11264], P('dp', 'tensor')
All inputs are finite; a program needn't handle non-finite values.
Results may differ from a plain program's by a relative error of at most 0.0087.
Values may be sent and summed in bfloat16 or wider, within the bound.
A program may use at most 64 MiB of HBM per device.

v0:
```python
import math
import jax
import jax.numpy as jnp
from jax import lax
from jax.sharding import PartitionSpec as P

FW = 11264
R = 512
beta_one = 0.9
beta_two = 0.999
adam_eps = 1e-08
corr_one = 1.0 - 0.9**10
corr_two = 1.0 - 0.999**10
step_size = 0.002
decay_keep = 0.99


def adam_update(lowrank, square, first_moment, second_moment):
    bound_norm = math.sqrt(R * FW)
    factor = jnp.minimum(1.0, bound_norm / (jnp.sqrt(square) + 1e-06))
    clipped = lowrank * factor
    first = beta_one * first_moment + (1.0 - beta_one) * clipped
    second = beta_two * second_moment + (1.0 - beta_two) * clipped * clipped
    update = (first / corr_one / (jnp.sqrt(second / corr_two) + adam_eps)).astype(jnp.bfloat16)
    return (first, second, update)


def on_device(inputs, out_grads, basis, weight, first_moment, second_moment):
    columns = lax.all_gather(basis, "dp", axis=0, tiled=True)
    regrouped = lax.all_to_all(columns, "tensor", split_axis=0, concat_axis=1, tiled=True)
    partial_value = jnp.dot(inputs, regrouped, preferred_element_type=jnp.float32)
    projected = lax.psum(partial_value, "tensor").astype(jnp.bfloat16)
    partial_low = lax.dot_general(
        projected, out_grads, (((0,), (0,)), ((), ())), preferred_element_type=jnp.float32
    )
    own_rows = lax.psum_scatter(partial_low, "dp", scatter_dimension=0, tiled=True)
    square = lax.psum(jnp.sum(own_rows * own_rows), ("dp", "tensor"))
    first, second, update = adam_update(own_rows, square, first_moment, second_moment)
    back_basis = lax.all_gather(basis, "tensor", axis=1, tiled=True)
    delta = jnp.dot(
        back_basis,
        lax.all_gather(update, "dp", axis=0, tiled=True),
        preferred_element_type=jnp.float32,
    )
    new_weight = (decay_keep * weight.astype(jnp.float32) - step_size * delta).astype(jnp.bfloat16)
    return (new_weight, first, second)


def solution(mesh):
    placed = (
        P("dp", "tensor"),
        P("dp", "tensor"),
        P("dp", "tensor"),
        P("dp", "tensor"),
        P("dp", "tensor"),
        P("dp", "tensor"),
    )
    return jax.shard_map(
        on_device,
        mesh=mesh,
        in_specs=placed,
        out_specs=(P("dp", "tensor"), P("dp", "tensor"), P("dp", "tensor")),
        check_vma=False,
    )
```

profile of v0, /device:TPU:0, one launch (start us, length us, event | category | flops | bytes accessed | tf_op | source)
XLA Modules:
  0.0 424.6 jit_solution(6178507596660154082)
XLA Ops:
  7.2 0.0 all-gather.3.cloned.1.call-start
  7.2 0.7 all-gather.3.cloned.1.call-update
  7.9 0.0 reduce-scatter.2.cloned.1.call-start
  7.9 55.3 %all-gather.3.cloned.1.call-done = bf16[8192,256]{1,0:T(8,128)(2,1)} async-done(((bf16[512,256]{1,0:T(8,128)(2,1)}), bf16[8192,256]{1,0:T(8,128)(2,1)}) %all-gather.3.cloned.1.call-update) | async-done | bytes 4194320 | tf_op jit(solution)/shard_map/all_gather | solution.py:29
  63.3 55.5 %all_to_all.19 = bf16[2,4096,256]{2,1,0:T(8,128)(2,1)} all-to-all(bf16[2,4096,256]{2,1,0:T(8,128)(2,1)} %bitcast.14), channel_id=1, replica_groups=mesh['dp'=16,'tensor'=2] {'tensor'}, dimensions={0} | all-to-all | bytes 8388608 | tf_op jit(solution)/shard_map/all_to_all | solution.py:30
  118.7 6.3 %copy.14 = bf16[4096,2,256]{0,2,1:T(8,128)(2,1)} copy(bf16[4096,2,256]{2,0,1:T(8,128)(2,1)} %bitcast.13) | data formatting | bytes 8388608 | tf_op jit(solution)/shard_map/all_to_all | solution.py:30
  125.0 5.9 %fusion.5 = f32[576,512]{1,0:T(8,128)S(1)} fusion(bf16[576,4096]{1,0:T(8,128)(2,1)} %param.6, bf16[4096,512]{0,1:T(8,128)(2,1)} %bitcast.15), kind=kOutput, calls=%fused_computation.9 | convolution fusion | flops 2415919104 | bytes 10092544 | tf_op jit(solution)/shard_map/dot_general | solution.py:31
  131.0 30.4 %all-reduce.1 = bf16[576,512]{1,0:T(8,128)(2,1)S(1)} all-reduce(f32[576,512]{1,0:T(8,128)S(1)} %fusion.5), channel_id=1, replica_groups=mesh['dp'=16,'tensor'=2] {'tensor'}, use_global_device_ids=true, to_apply=%region_0.0 | all-reduce | flops 294912 | bytes 1769472 | tf_op jit(solution)/shard_map/psum | solution.py:32
  161.4 10.3 %fusion.6 = f32[512,5632]{1,0:T(8,128)} fusion(bf16[576,512]{1,0:T(8,128)(2,1)S(1)} %all-reduce.1, bf16[576,5632]{1,0:T(8,128)(2,1)} %param.7), kind=kOutput, calls=%fused_computation.10 | convolution fusion | flops 3321888768 | bytes 18612224 | tf_op jit(solution)/shard_map/dot_general | solution.py:33
  171.7 0.0 copy-start.1
  171.7 0.0 copy-start.2
  171.7 0.0 reduce-scatter.2.cloned.1.call-update
  171.8 0.0 all-gather.5.cloned.1.call-start
  171.8 125.4 %reduce-scatter.2.cloned.1.call-done = f32[32,5632]{1,0:T(8,128)} async-done(((f32[512,5632]{1,0:T(8,128)}), f32[32,5632]{1,0:T(8,128)}) %reduce-scatter.2.cloned.1.call-update) | async-done | bytes 720912 | tf_op jit(solution)/shard_map/reduce_scatter | solution.py:36
  297.2 1.9 multiply_reduce_fusion
  299.1 39.9 %psum.15 = f32[]{:T(128)} all-reduce(f32[]{:T(128)} %multiply_reduce_fusion), channel_id=1, replica_groups=mesh['dp'=16,'tensor'=2] {'dp','tensor'}, use_global_device_ids=true, to_apply=%region_3.0 | all-reduce | flops 1 | bytes 8 | tf_op jit(solution)/shard_map/psum | solution.py:37
  339.7 0.0 copy-done.1
  339.8 0.0 copy-done.2
  339.8 2.6 divide_convert_fusion
  342.4 0.0 all-gather.5.cloned.1.call-update
  342.4 0.0 copy-start
  342.4 8.4 %copy.13 = bf16[512,5632]{0,1:T(8,128)(2,1)} copy(bf16[512,5632]{1,0:T(8,128)(2,1)} %param.9) | data formatting | bytes 11534336 | tf_op args[3]
  350.8 0.0 copy-done
  350.8 8.0 %all_gather.11 = bf16[512,512]{1,0:T(8,128)(2,1)S(1)} all-gather(bf16[512,256]{1,0:T(8,128)(2,1)S(1)} %copy-done), channel_id=1, replica_groups=mesh['dp'=16,'tensor'=2] {'tensor'}, dimensions={1}, use_global_device_ids=true | all-gather | bytes 786432 | tf_op jit(solution)/shard_map/all_gather | solution.py:39
  358.8 42.2 %all-gather.5.cloned.1.call-done = bf16[512,5632]{1,0:T(8,128)(2,1)} async-done(((bf16[32,5632]{1,0:T(8,128)(2,1)}), bf16[512,5632]{1,0:T(8,128)(2,1)}) %all-gather.5.cloned.1.call-update) | async-done | bytes 5767184 | tf_op jit(solution)/shard_map/all_gather | solution.py:42
  401.0 8.7 %fusion = bf16[512,5632]{0,1:T(8,128)(2,1)} fusion(bf16[512,5632]{0,1:T(8,128)(2,1)} %copy.13, bf16[512,5632]{1,0:T(8,128)(2,1)} %all-gather.5.cloned.1.call-done, bf16[512,512]{1,0:T(8,128)(2,1)S(1)} %all_gather.11), kind=kOutput, calls=%fused_computation.1 | convolution fusion | flops 2967207936 | bytes 17825792 | tf_op jit(solution)/shard_map/dot_general | solution.py:40
  409.7 8.4 %copy.15 = bf16[512,5632]{1,0:T(8,128)(2,1)} copy(bf16[512,5632]{0,1:T(8,128)(2,1)} %fusion) | data formatting | bytes 11534336
Async XLA Ops:
  7.2 56.1 %all-gather.3.cloned.1.call-start = ((), (), s32[]{:S(2)}) async-start(), calls=%async_computation.2 | async-start | bytes 4456448 | tf_op jit(solution)/shard_map/all_gather | solution.py:29
  7.9 289.3 %reduce-scatter.2.cloned.1.call-start = ((), (), s32[]{:S(2)}) async-start(), calls=%async_computation.3 | async-start | bytes 12255232 | tf_op jit(solution)/shard_map/reduce_scatter | solution.py:36
  171.7 168.0 %copy-start.1 = (f32[32,5632]{1,0:T(8,128)S(1)}, f32[32,5632]{1,0:T(8,128)}, u32[]{:S(2)}) copy-start(f32[32,5632]{1,0:T(8,128)} %param.10) | copy-start | bytes 2162692
  171.7 168.0 %copy-start.2 = (f32[32,5632]{1,0:T(8,128)S(1)}, f32[32,5632]{1,0:T(8,128)}, u32[]{:S(2)}) copy-start(f32[32,5632]{1,0:T(8,128)} %param.11) | copy-start | bytes 2162692
  171.8 229.3 %all-gather.5.cloned.1.call-start = ((), (), s32[]{:S(2)}) async-start(), calls=%async_computation.4 | async-start | bytes 6127616 | tf_op jit(solution)/shard_map/all_gather | solution.py:42
  342.4 8.4 %copy-start = (bf16[512,256]{1,0:T(8,128)(2,1)S(1)}, bf16[512,256]{1,0:T(8,128)(2,1)}, u32[]{:S(2)}) copy-start(bf16[512,256]{1,0:T(8,128)(2,1)} %param.8) | copy-start | bytes 786436
Sparse Core Ops, SparseCore 0:
  10.1 53.0 all-gather.2
  171.9 125.2 reduce-scatter.1
  342.5 58.4 all-gather.4
where the time goes:
time: 426 us; the launch traced here: 425 us
  waiting for transfers between devices  224 us (53%)
  blocking collectives  134 us (31%)
  matrix products  24.9 us (6%)
  local copies, waits for them, and re-layouts  23.1 us (5%)
  between operations  14.5 us (3%)
  other arithmetic  4.48 us (1%)
    reduce_scatter x1, waiting for transfers between devices, on_device(): lax.psum_scatter(partial_low, 'dp', scatter_dimension=0, tiled=True)  125 us
    all_to_all x1, blocking collectives, on_device(): lax.all_to_all(columns, 'tensor', split_axis=0, concat_axis=1, tiled=True)  55.5 us
    all_gather x1, waiting for transfers between devices, on_device(): columns = lax.all_gather(basis, 'dp', axis=0, tiled=True)  55.3 us
    all_gather x1, waiting for transfers between devices, on_device(): lax.all_gather(update, 'dp', axis=0, tiled=True)  42.2 us
    psum x1, blocking collectives, on_device(): square = lax.psum(jnp.sum(own_rows * own_rows), ('dp', 'tensor'))  39.9 us
    psum x1, blocking collectives, on_device(): projected = lax.psum(partial_value, 'tensor').astype(jnp.bfloat16)  30.4 us
    unnamed x8, local copies, waits for them, and re-layouts  16.8 us
    dot_general x1, matrix products, on_device(): lax.dot_general(projected, out_grads, (((0,), (0,)), ((), ())), preferred...  10.3 us
  transfers between devices with their start and end apart: 3, of which 3 were waited for; matrix products, arithmetic and copies ran while one was open for 2% of the time, Pallas kernels for 0%

commit v1 on v0

--- a/solution.py
+++ b/solution.py
@@ -29,7 +29,9 @@
     columns = lax.all_gather(basis, "dp", axis=0, tiled=True)
     regrouped = lax.all_to_all(columns, "tensor", split_axis=0, concat_axis=1, tiled=True)
     partial_value = jnp.dot(inputs, regrouped, preferred_element_type=jnp.float32)
-    projected = lax.psum(partial_value, "tensor").astype(jnp.bfloat16)
+    projected = (partial_value + lax.ppermute(partial_value, "tensor", [(0, 1), (1, 0)])).astype(
+        jnp.bfloat16
+    )
     partial_low = lax.dot_general(
         projected, out_grads, (((0,), (0,)), ((), ())), preferred_element_type=jnp.float32
     )

time: 426 us -> 419 us (0.984)
  blocking collectives: 134 us -> 103 us
  waiting for transfers between devices: 224 us -> 250 us
    psum x1 -> x0, blocking collectives: 30.4 us -> none  [on_device(): projected = lax.psum(partial_value, 'tensor').astype(jnp.bfloat16)]
    ppermute x0 -> x1, waiting for transfers between devices: none -> 27 us  [on_device(): lax.ppermute(partial_value, 'tensor', [(0, 1), (1, 0)])]
    unnamed x8 -> x12, local copies, waits for them, and re-layouts: 16.8 us -> 16.8 us
  transfers between devices with their start and end apart: 3 -> 4, of which waited for: 3 -> 4; matrix products, arithmetic and copies ran while one was open for 2% -> 2% of each run, Pallas kernels for 0% -> 0%
where the time goes in v1:
time: 419 us
  waiting for transfers between devices  250 us (60%)
  blocking collectives  103 us (25%)
  local copies, waits for them, and re-layouts  23.2 us (6%)
  matrix products  22.5 us (5%)
  between operations  14.5 us (3%)
  other arithmetic  4.49 us (1%)
    reduce_scatter x1, waiting for transfers between devices, on_device(): lax.psum_scatter(partial_low, 'dp', scatter_dimension=0, tiled=True)  125 us
    all_to_all x1, blocking collectives, on_device(): lax.all_to_all(columns, 'tensor', split_axis=0, concat_axis=1, tiled=True)  55.4 us
    all_gather x1, waiting for transfers between devices, on_device(): columns = lax.all_gather(basis, 'dp', axis=0, tiled=True)  55.3 us
    all_gather x1, waiting for transfers between devices, on_device(): lax.all_gather(update, 'dp', axis=0, tiled=True)  42.2 us
    psum x1, blocking collectives, on_device(): square = lax.psum(jnp.sum(own_rows * own_rows), ('dp', 'tensor'))  39.9 us
    ppermute x1, waiting for transfers between devices, on_device(): lax.ppermute(partial_value, 'tensor', [(0, 1), (1, 0)])  27 us
    unnamed x12, local copies, waits for them, and re-layouts  16.8 us
    dot_general x1, matrix products, on_device(): jnp.dot(back_basis, lax.all_gather(update, 'dp', axis=0, tiled=True), pre...  8.65 us
  transfers between devices with their start and end apart: 4, of which 4 were waited for; matrix products, arithmetic and copies ran while one was open for 2% of the time, Pallas kernels for 0%

profile of v1, /device:TPU:0, one launch (start us, length us, event | category | flops | bytes accessed | tf_op | source)
XLA Modules:
  0.0 418.5 jit_solution(3194111342149376009)
XLA Ops:
  7.2 0.0 all-gather.3.cloned.1.call-start
  7.2 0.7 all-gather.3.cloned.1.call-update
  7.9 0.0 reduce-scatter.2.cloned.1.call-start
  7.9 55.3 %all-gather.3.cloned.1.call-done = bf16[8192,256]{1,0:T(8,128)(2,1)} async-done(((bf16[512,256]{1,0:T(8,128)(2,1)}), bf16[8192,256]{1,0:T(8,128)(2,1)}) %all-gather.3.cloned.1.call-update) | async-done | bytes 4194320 | tf_op jit(solution)/shard_map/all_gather | solution.py:29
  63.3 55.4 %all_to_all.19 = bf16[2,4096,256]{2,1,0:T(8,128)(2,1)} all-to-all(bf16[2,4096,256]{2,1,0:T(8,128)(2,1)} %bitcast.15), channel_id=1, replica_groups=mesh['dp'=16,'tensor'=2] {'tensor'}, dimensions={0} | all-to-all | bytes 8388608 | tf_op jit(solution)/shard_map/all_to_all | solution.py:30
  118.7 0.0 slice-start
  118.7 6.5 %copy.14 = bf16[4096,2,256]{0,2,1:T(8,128)(2,1)} copy(bf16[4096,2,256]{2,0,1:T(8,128)(2,1)} %bitcast.12) | data formatting | bytes 8388608 | tf_op jit(solution)/shard_map/all_to_all | solution.py:30
  125.2 0.0 slice-start.1
  125.2 6.1 %fusion.4 = f32[576,512]{1,0:T(8,128)S(1)} fusion(bf16[576,4096]{1,0:T(8,128)(2,1)} %param.6, bf16[4096,512]{0,1:T(8,128)(2,1)} %bitcast.16), kind=kOutput, calls=%fused_computation.9 | convolution fusion | flops 2415919104 | bytes 10092544 | tf_op jit(solution)/shard_map/dot_general | solution.py:31
  131.3 0.4 collective-permute-start
  131.6 27.0 %collective-permute-done = f32[576,512]{1,0:T(8,128)S(1)} collective-permute-done((f32[576,512]{1,0:T(8,128)S(1)}, f32[576,512]{1,0:T(8,128)S(1)}, u32[]{:S(2)}, u32[]{:S(2)}) %collective-permute-start) | collective-permute-done | bytes 1179680 | tf_op jit(solution)/shard_map/ppermute | solution.py:32
  158.6 0.0 slice-done
  158.6 0.0 slice-done.1
  158.6 7.7 %fusion.2 = f32[512,5632]{1,0:T(8,128)} fusion(bf16[576,5632]{1,0:T(8,128)(2,1)S(1)} %bitcast.14, f32[576,512]{1,0:T(8,128)S(1)} %fusion.4, f32[576,512]{1,0:T(8,128)S(1)} %collective-permute-done), kind=kOutput, calls=%fused_computation.8 | convolution fusion | flops 3322478592 | bytes 20381696 | tf_op jit(solution)/shard_map/dot_general | solution.py:35
  166.3 0.0 copy-start.1
  166.3 0.0 copy-start.2
  166.3 0.0 reduce-scatter.2.cloned.1.call-update
  166.4 0.0 all-gather.5.cloned.1.call-start
  166.4 124.8 %reduce-scatter.2.cloned.1.call-done = f32[32,5632]{1,0:T(8,128)} async-done(((f32[512,5632]{1,0:T(8,128)}), f32[32,5632]{1,0:T(8,128)}) %reduce-scatter.2.cloned.1.call-update) | async-done | bytes 720912 | tf_op jit(solution)/shard_map/reduce_scatter | solution.py:38
  291.2 1.9 multiply_reduce_fusion
  293.1 39.9 %psum.7 = f32[]{:T(128)} all-reduce(f32[]{:T(128)} %multiply_reduce_fusion), channel_id=1, replica_groups=mesh['dp'=16,'tensor'=2] {'dp','tensor'}, use_global_device_ids=true, to_apply=%region_2.0 | all-reduce | flops 1 | bytes 8 | tf_op jit(solution)/shard_map/psum | solution.py:39
  333.7 0.0 copy-done.1
  333.7 0.0 copy-done.2
  333.7 2.6 divide_convert_fusion
  336.3 0.0 all-gather.5.cloned.1.call-update
  336.3 0.0 copy-start
  336.4 8.4 %copy.13 = bf16[512,5632]{0,1:T(8,128)(2,1)} copy(bf16[512,5632]{1,0:T(8,128)(2,1)} %param.9) | data formatting | bytes 11534336 | tf_op args[3]
  344.8 0.0 copy-done
  344.8 8.0 %all_gather.11 = bf16[512,512]{1,0:T(8,128)(2,1)S(1)} all-gather(bf16[512,256]{1,0:T(8,128)(2,1)S(1)} %copy-done), channel_id=1, replica_groups=mesh['dp'=16,'tensor'=2] {'tensor'}, dimensions={1}, use_global_device_ids=true | all-gather | bytes 786432 | tf_op jit(solution)/shard_map/all_gather | solution.py:41
  352.8 42.2 %all-gather.5.cloned.1.call-done = bf16[512,5632]{1,0:T(8,128)(2,1)} async-done(((bf16[32,5632]{1,0:T(8,128)(2,1)}), bf16[512,5632]{1,0:T(8,128)(2,1)}) %all-gather.5.cloned.1.call-update) | async-done | bytes 5767184 | tf_op jit(solution)/shard_map/all_gather | solution.py:44
  395.0 8.6 %fusion = bf16[512,5632]{0,1:T(8,128)(2,1)} fusion(bf16[512,5632]{0,1:T(8,128)(2,1)} %copy.13, bf16[512,5632]{1,0:T(8,128)(2,1)} %all-gather.5.cloned.1.call-done, bf16[512,512]{1,0:T(8,128)(2,1)S(1)} %all_gather.11), kind=kOutput, calls=%fused_computation.1 | convolution fusion | flops 2967207936 | bytes 17825792 | tf_op jit(solution)/shard_map/dot_general | solution.py:42
  403.7 8.4 %copy.15 = bf16[512,5632]{1,0:T(8,128)(2,1)} copy(bf16[512,5632]{0,1:T(8,128)(2,1)} %fusion) | data formatting | bytes 11534336
  (1 shorter events, 0.0 us)
Async XLA Ops:
  7.2 56.1 %all-gather.3.cloned.1.call-start = ((), (), s32[]{:S(2)}) async-start(), calls=%async_computation.2 | async-start | bytes 4456448 | tf_op jit(solution)/shard_map/all_gather | solution.py:29
  7.9 283.3 %reduce-scatter.2.cloned.1.call-start = ((), (), s32[]{:S(2)}) async-start(), calls=%async_computation.3 | async-start | bytes 12255232 | tf_op jit(solution)/shard_map/reduce_scatter | solution.py:38
  118.7 39.9 %slice-start = ((s8[6488064]{0:T(1024)(128)(4,1)}), s8[2293760]{0:T(1024)(128)(4,1)S(1)}, s32[]{:S(2)}) async-start(s8[6488064]{0:T(1024)(128)(4,1)} %bitcast.13), calls=%async_computation.5 | async-start | bytes 4587520
  125.2 33.4 %slice-start.1 = ((s8[6488064]{0:T(1024)(128)(4,1)}), s8[4194304]{0:T(1024)(128)(4,1)S(1)}, s32[]{:S(2)}) async-start(s8[6488064]{0:T(1024)(128)(4,1)} %bitcast.13), calls=%async_computation.6 | async-start | bytes 8388608
  131.3 27.3 %collective-permute-start = (f32[576,512]{1,0:T(8,128)S(1)}, f32[576,512]{1,0:T(8,128)S(1)}, u32[]{:S(2)}, u32[]{:S(2)}) collective-permute-start(f32[576,512]{1,0:T(8,128)S(1)} %fusion.4), channel_id=1, source_target_pairs={{0,1},{1,0},{2,3},{3,2},{4,5},{5,4},{6,7},{7,6},{8,9},{9,8},{10,11... | collective-permute-start | bytes 3538952 | tf_op jit(solution)/shard_map/ppermute | solution.py:32
  166.3 167.4 %copy-start.1 = (f32[32,5632]{1,0:T(8,128)S(1)}, f32[32,5632]{1,0:T(8,128)}, u32[]{:S(2)}) copy-start(f32[32,5632]{1,0:T(8,128)} %param.10) | copy-start | bytes 2162692
  166.3 167.4 %copy-start.2 = (f32[32,5632]{1,0:T(8,128)S(1)}, f32[32,5632]{1,0:T(8,128)}, u32[]{:S(2)}) copy-start(f32[32,5632]{1,0:T(8,128)} %param.11) | copy-start | bytes 2162692
  166.4 228.7 %all-gather.5.cloned.1.call-start = ((), (), s32[]{:S(2)}) async-start(), calls=%async_computation.4 | async-start | bytes 6127616 | tf_op jit(solution)/shard_map/all_gather | solution.py:44
  336.3 8.4 %copy-start = (bf16[512,256]{1,0:T(8,128)(2,1)S(1)}, bf16[512,256]{1,0:T(8,128)(2,1)}, u32[]{:S(2)}) copy-start(bf16[512,256]{1,0:T(8,128)(2,1)} %param.8) | copy-start | bytes 786436
Sparse Core Ops, SparseCore 0:
  10.1 53.0 all-gather.2
  166.5 124.6 reduce-scatter.1
  336.5 58.4 all-gather.4
